TPU v7x, 256 devices: a whole 4x4x8 slice. The times are simulated.
256 devices in a mesh: param: 64 (over z, x, core), ex: 4 (over y).
Axes of the slice: x: 4, y: 4, z: 8, core: 2. Of those that a mesh axis runs over, the one named last changes fastest.
Arguments:
- gradients: bfloat16 [512, 524288], P('ex', 'param'), may hold values from -60 to 60
- projection_seed: int32 [1], replicated, may hold values from 0 to 1048575
- target_features: bfloat16 [512, 4096], replicated, may hold values from -0.09375 to 0.09375
Outputs:
- scores: float32 [512, 512], P('param', 'ex')
All inputs are finite; a program needn't handle non-finite values.
Results may differ from a plain program's by a relative error of at most 0.011.
Values may be sent and summed in bfloat16 or wider, within the bound.
No kernel may reach another device: no remote copies, remote signals or barrier semaphores. Data moves between devices by JAX's collectives and lax.ppermute only.
A program may use at most 64 MiB of HBM per device.

v0:
```python
import math
import jax
import jax.numpy as jnp
from jax import lax
from jax.sharding import PartitionSpec as P

FEATS = 4096
BLOCK = 128
STEPS = 10
DAMPING = 0.001


def partner_2(array, axis, distance):
    return lax.ppermute(array, axis, [(i, i ^ 1 << distance) for i in range(lax.axis_size(axis))])


def hashed(seed_value, row_start, row_count, col_start, col_count, total_coords):
    row_index = (row_start + lax.iota(jnp.int32, row_count)).reshape(row_count, 1)
    col_index = (col_start + lax.iota(jnp.int32, col_count)).reshape(1, col_count)
    mixed = row_index * 73856093 ^ col_index * 19349663 ^ seed_value * 83492791
    mixed = mixed ^ jnp.right_shift(mixed, 13)
    mixed = mixed * 1274126177
    mixed = mixed ^ jnp.right_shift(mixed, 16)
    uniform_value = (mixed & 65535).astype(jnp.float32) * (1.0 / 65536.0)
    return ((2.0 * uniform_value - 1.0) * math.sqrt(3.0 / total_coords)).astype(jnp.bfloat16)


def newton_inverse(fisher):
    width = fisher.shape[1]
    identity = jnp.eye(width, dtype=jnp.float32)
    trace_value = jnp.einsum("bii->b", fisher)
    damped = fisher + (DAMPING * trace_value)[:, None, None] * identity
    total = jnp.einsum("bii->b", damped)
    iterate = identity[None] / total[:, None, None]
    for _ in range(STEPS):
        product = jnp.einsum("bij,bjk->bik", damped, iterate, precision=lax.Precision.HIGHEST)
        iterate = jnp.einsum(
            "bij,bjk->bik", iterate, 2.0 * identity - product, precision=lax.Precision.HIGHEST
        )
    return iterate


def to_targets(partial_scores):
    return lax.all_to_all(partial_scores, "param", split_axis=0, concat_axis=1, tiled=True)


def on_device(gradients, projection_seed, target_features):
    seed_value = projection_seed[0]
    my_index = lax.axis_index("param")
    param_count = lax.axis_size("param")
    exam_dev, coord_dev = gradients.shape
    total_coords = coord_dev * param_count
    row_start = my_index * coord_dev
    examples_total = exam_dev * lax.axis_size("ex")
    feats_owned = FEATS // param_count
    piece_width = math.gcd(feats_owned * lax.axis_size("param"), 512)

    def project_piece(col_start):
        matrix = hashed(seed_value, row_start, coord_dev, col_start, piece_width, total_coords)
        return jnp.dot(gradients, matrix, preferred_element_type=jnp.float32).T

    starts = piece_width * lax.iota(jnp.int32, feats_owned * lax.axis_size("param") // piece_width)
    pieces = lax.map(project_piece, starts)
    owned = lax.psum_scatter(
        pieces.reshape(feats_owned * lax.axis_size("param"), exam_dev),
        "param",
        scatter_dimension=0,
        tiled=True,
    ).astype(jnp.bfloat16)
    partner = partner_2(owned, "param", 0)
    is_lower = my_index % 2 == 0
    block_rows = jnp.concatenate(
        [jnp.where(is_lower, owned, partner), jnp.where(is_lower, partner, owned)], 0
    )
    block_total = block_rows.shape[0] // BLOCK
    blocks = block_rows.reshape(block_total, BLOCK, exam_dev)
    partial_fisher = jnp.einsum("bie,bje->bij", blocks, blocks, preferred_element_type=jnp.float32)
    fisher = lax.psum(partial_fisher, "ex") / examples_total
    inverse_bf = newton_inverse(fisher).astype(jnp.bfloat16)
    conditioned = jnp.einsum("bmj,bme->bje", inverse_bf, blocks, preferred_element_type=jnp.float32)
    conditioned = conditioned.astype(jnp.bfloat16).reshape(block_rows.shape[0], exam_dev)
    conditioned = lax.dynamic_slice_in_dim(conditioned, my_index % 2 * feats_owned, feats_owned, 0)
    example_rows = lax.all_to_all(conditioned, "param", split_axis=1, concat_axis=0, tiled=True)
    return to_targets(jnp.dot(target_features, example_rows, preferred_element_type=jnp.float32))


def solution(mesh):
    placed = (P("ex", "param"), P(), P())
    return jax.shard_map(
        on_device, mesh=mesh, in_specs=placed, out_specs=P("param", "ex"), check_vma=False
    )
```

profile of v0, /device:TPU:1, one launch (start us, length us, event | category | flops | bytes accessed | tf_op | source)
XLA Modules:
  0.0 352.5 jit_solution(12516402552739975225)
XLA Ops:
  7.2 89.3 %while.12 = (s32[]{:T(128)}, f32[8,512,128]{2,1,0:T(8,128)}, s32[]{:T(128)}, s32[8]{0:T(128)S(1)}, s32[]{:T(128)}, /*index=5*/bf16[128,8192]{1,0:T(8,128)(2,1)}, s32[]{:T(128)}) while((s32[]{:T(128)}, f32[8,512,128]{2,1,0:T(8,128)}, s32[]{:T(128)}, s32[8]{0:T(128)S(1)}, s32[]{:T(128)}, /*index=5*/bf16[128,8192]{1,0:T(8,128)(2,1)}, ...), condition=%wide.region_1.2_spmd, body=%wide.region_0.1_spmd.sunk | while | flops 1128285184 | bytes 2430049 | solution.py:63
  7.2 0.6 dynamic_slice.9
  7.8 0.6 add_multiply_fusion.4
  8.4 9.9 %fusion.89 = f32[8,512,128]{2,1,0:T(8,128)} fusion(f32[8,512,128]{2,1,0:T(8,128)} %get-tuple-element.145, s32[]{:T(128)} %get-tuple-element.144, bf16[128,8192]{1,0:T(8,128)(2,1)} %get-tuple-element.156, s32[]{:T(128)} %get-tuple-element.155, s32[512]{0:T(512)S(1)} %add_multiply_fusion.4, s32[8192]{0:T(1024)S(1)} %add_multiply_fusion.5), kind=kOutput, calls=%fused_computation.11.clone.1 | convolution fusion | flops 1128267776 | bytes 2395136 | tf_op jit(solution)/shard_map/while/body/eval_jaxpr/dot_general | solution.py:60
  18.4 0.6 dynamic_slice.9
  18.9 0.6 add_multiply_fusion.4
  19.6 9.9 %fusion.89 = f32[8,512,128]{2,1,0:T(8,128)} fusion(f32[8,512,128]{2,1,0:T(8,128)} %get-tuple-element.145, s32[]{:T(128)} %get-tuple-element.144, bf16[128,8192]{1,0:T(8,128)(2,1)} %get-tuple-element.156, s32[]{:T(128)} %get-tuple-element.155, s32[512]{0:T(512)S(1)} %add_multiply_fusion.4, s32[8192]{0:T(1024)S(1)} %add_multiply_fusion.5), kind=kOutput, calls=%fused_computation.11.clone.1 | convolution fusion | flops 1128267776 | bytes 2395136 | tf_op jit(solution)/shard_map/while/body/eval_jaxpr/dot_general | solution.py:60
  29.5 0.6 dynamic_slice.9
  30.1 0.6 add_multiply_fusion.4
  30.7 9.9 %fusion.89 = f32[8,512,128]{2,1,0:T(8,128)} fusion(f32[8,512,128]{2,1,0:T(8,128)} %get-tuple-element.145, s32[]{:T(128)} %get-tuple-element.144, bf16[128,8192]{1,0:T(8,128)(2,1)} %get-tuple-element.156, s32[]{:T(128)} %get-tuple-element.155, s32[512]{0:T(512)S(1)} %add_multiply_fusion.4, s32[8192]{0:T(1024)S(1)} %add_multiply_fusion.5), kind=kOutput, calls=%fused_computation.11.clone.1 | convolution fusion | flops 1128267776 | bytes 2395136 | tf_op jit(solution)/shard_map/while/body/eval_jaxpr/dot_general | solution.py:60
  40.7 0.6 dynamic_slice.9
  41.2 0.6 add_multiply_fusion.4
  41.9 9.9 %fusion.89 = f32[8,512,128]{2,1,0:T(8,128)} fusion(f32[8,512,128]{2,1,0:T(8,128)} %get-tuple-element.145, s32[]{:T(128)} %get-tuple-element.144, bf16[128,8192]{1,0:T(8,128)(2,1)} %get-tuple-element.156, s32[]{:T(128)} %get-tuple-element.155, s32[512]{0:T(512)S(1)} %add_multiply_fusion.4, s32[8192]{0:T(1024)S(1)} %add_multiply_fusion.5), kind=kOutput, calls=%fused_computation.11.clone.1 | convolution fusion | flops 1128267776 | bytes 2395136 | tf_op jit(solution)/shard_map/while/body/eval_jaxpr/dot_general | solution.py:60
  51.8 0.6 dynamic_slice.9
  52.4 0.6 add_multiply_fusion.4
  53.0 9.9 %fusion.89 = f32[8,512,128]{2,1,0:T(8,128)} fusion(f32[8,512,128]{2,1,0:T(8,128)} %get-tuple-element.145, s32[]{:T(128)} %get-tuple-element.144, bf16[128,8192]{1,0:T(8,128)(2,1)} %get-tuple-element.156, s32[]{:T(128)} %get-tuple-element.155, s32[512]{0:T(512)S(1)} %add_multiply_fusion.4, s32[8192]{0:T(1024)S(1)} %add_multiply_fusion.5), kind=kOutput, calls=%fused_computation.11.clone.1 | convolution fusion | flops 1128267776 | bytes 2395136 | tf_op jit(solution)/shard_map/while/body/eval_jaxpr/dot_general | solution.py:60
  63.0 0.6 dynamic_slice.9
  63.6 0.6 add_multiply_fusion.4
  64.2 9.9 %fusion.89 = f32[8,512,128]{2,1,0:T(8,128)} fusion(f32[8,512,128]{2,1,0:T(8,128)} %get-tuple-element.145, s32[]{:T(128)} %get-tuple-element.144, bf16[128,8192]{1,0:T(8,128)(2,1)} %get-tuple-element.156, s32[]{:T(128)} %get-tuple-element.155, s32[512]{0:T(512)S(1)} %add_multiply_fusion.4, s32[8192]{0:T(1024)S(1)} %add_multiply_fusion.5), kind=kOutput, calls=%fused_computation.11.clone.1 | convolution fusion | flops 1128267776 | bytes 2395136 | tf_op jit(solution)/shard_map/while/body/eval_jaxpr/dot_general | solution.py:60
  74.2 0.6 dynamic_slice.9
  74.7 0.6 add_multiply_fusion.4
  75.4 9.9 %fusion.89 = f32[8,512,128]{2,1,0:T(8,128)} fusion(f32[8,512,128]{2,1,0:T(8,128)} %get-tuple-element.145, s32[]{:T(128)} %get-tuple-element.144, bf16[128,8192]{1,0:T(8,128)(2,1)} %get-tuple-element.156, s32[]{:T(128)} %get-tuple-element.155, s32[512]{0:T(512)S(1)} %add_multiply_fusion.4, s32[8192]{0:T(1024)S(1)} %add_multiply_fusion.5), kind=kOutput, calls=%fused_computation.11.clone.1 | convolution fusion | flops 1128267776 | bytes 2395136 | tf_op jit(solution)/shard_map/while/body/eval_jaxpr/dot_general | solution.py:60
  85.3 0.6 dynamic_slice.9
  85.9 0.6 add_multiply_fusion.4
  86.5 9.9 %fusion.89 = f32[8,512,128]{2,1,0:T(8,128)} fusion(f32[8,512,128]{2,1,0:T(8,128)} %get-tuple-element.145, s32[]{:T(128)} %get-tuple-element.144, bf16[128,8192]{1,0:T(8,128)(2,1)} %get-tuple-element.156, s32[]{:T(128)} %get-tuple-element.155, s32[512]{0:T(512)S(1)} %add_multiply_fusion.4, s32[8192]{0:T(1024)S(1)} %add_multiply_fusion.5), kind=kOutput, calls=%fused_computation.11.clone.1 | convolution fusion | flops 1128267776 | bytes 2395136 | tf_op jit(solution)/shard_map/while/body/eval_jaxpr/dot_general | solution.py:60
  96.5 0.0 all-reduce.2.cloned.1.call-start
  96.5 140.2 %reduce-scatter.2.cloned.1.call-done = f32[64,128]{1,0:T(8,128)} async-done(((f32[4096,128]{1,0:T(8,128)}), f32[64,128]{1,0:T(8,128)}) %reduce-scatter.2.cloned.1.call-update) | async-done | bytes 32784 | tf_op jit(solution)/shard_map/reduce_scatter | solution.py:64
  236.7 0.8 convert_element_type.28
  237.5 5.9 %collective-permute-start = (bf16[64,128]{1,0:T(8,128)(2,1)S(1)}, bf16[64,128]{1,0:T(8,128)(2,1)S(1)}, u32[]{:S(2)}, u32[]{:S(2)}) collective-permute-start(bf16[64,128]{1,0:T(8,128)(2,1)S(1)} %convert_element_type.28), channel_id=1, source_target_pairs={{0,4},{4,0},{8,12},{12,8},{16,20},{20,16},{24,28},{28,24},{32,36},... | collective-permute-start | bytes 49160 | tf_op jit(solution)/shard_map/ppermute | solution.py:14
  243.4 0.8 collective-permute-done
  244.2 0.8 broadcast_select_fusion.1
  245.0 0.8 convolution_bitcast_fusion
  245.8 42.4 %all-reduce.2.cloned.1.call-done = f32[1,128,128]{2,1,0:T(8,128)} async-done(((f32[1,128,128]{2,1,0:T(8,128)}), f32[1,128,128]{2,1,0:T(8,128)}) %all-reduce.2.cloned.1.call-update) | async-done | bytes 65552 | tf_op jit(solution)/shard_map/psum | solution.py:78
  288.2 1.5 select_reduce_fusion.1
  290.3 1.5 select_reduce_fusion
  292.5 1.0 convolution_subtract_fusion.9
  293.5 0.2 fusion.22
  293.7 1.0 convolution_subtract_fusion.8
  294.8 0.2 fusion.44
  295.0 1.0 convolution_subtract_fusion.7
  296.0 0.2 fusion.45
  296.3 1.0 convolution_subtract_fusion.6
  297.3 0.2 fusion.46
  297.5 1.0 convolution_subtract_fusion.5
  298.6 0.2 fusion.47
  298.8 1.0 convolution_subtract_fusion.4
  299.8 0.2 fusion.48
  300.1 1.0 convolution_subtract_fusion.3
  301.1 0.2 fusion.49
  301.3 1.0 convolution_subtract_fusion.2
  302.4 0.2 fusion.50
  302.6 1.0 convolution_subtract_fusion.1
  303.6 0.2 fusion.51
  303.9 1.0 convolution_subtract_fusion
  304.9 0.2 convolution_convert_fusion
  305.1 0.2 fusion.39
  305.3 0.1 copy.9
  305.4 21.9 %all_to_all.38 = bf16[64,64,2]{0,2,1:T(2,128)(2,1)S(1)} all-to-all(bf16[64,64,2]{0,2,1:T(2,128)(2,1)S(1)} %bitcast.81), channel_id=1, replica_groups=mesh['param'=64,'ex'=4] {'param'}, dimensions={1} | all-to-all | bytes 32768 | tf_op jit(solution)/shard_map/all_to_all | solution.py:83
  327.3 0.1 all_to_all.31
  327.4 3.4 convolution_bitcast_fusion.1
  330.8 0.1 all_to_all.32
  330.9 0.1 copy.11
  331.0 14.0 %all_to_all.39 = f32[64,8,2]{1,2,0:T(2,128)S(1)} all-to-all(f32[64,8,2]{1,2,0:T(2,128)S(1)} %copy.11), channel_id=1, replica_groups=mesh['param'=64,'ex'=4] {'param'}, dimensions={0} | all-to-all | bytes 8192 | tf_op jit(solution)/shard_map/all_to_all | solution.py:44
  345.0 0.7 copy.12
  (15 shorter events, 0.1 us)
Async XLA Ops:
  6.5 230.2 %reduce-scatter.2.cloned.1.call-start = ((), (), s32[]{:S(2)}) async-start(), calls=%async_computation.3 | async-start | bytes 2129920 | tf_op jit(solution)/shard_map/reduce_scatter | solution.py:64
  96.5 191.7 %all-reduce.2.cloned.1.call-start = ((), (), s32[]{:S(2)}) async-start(), calls=%async_computation.4 | async-start | bytes 131072 | tf_op jit(solution)/shard_map/psum | solution.py:78
  237.5 6.7 %collective-permute-start = (bf16[64,128]{1,0:T(8,128)(2,1)S(1)}, bf16[64,128]{1,0:T(8,128)(2,1)S(1)}, u32[]{:S(2)}, u32[]{:S(2)}) collective-permute-start(bf16[64,128]{1,0:T(8,128)(2,1)S(1)} %convert_element_type.28), channel_id=1, source_target_pairs={{0,4},{4,0},{8,12},{12,8},{16,20},{20,16},{24,28},{28,24},{32,36},... | collective-permute-start | bytes 49160 | tf_op jit(solution)/shard_map/ppermute | solution.py:14
Sparse Core Ops, SparseCore 0:
  96.6 140.0 reduce-scatter.1
  245.9 42.2 all-reduce.1
where the time goes:
time: 354 us; the launch traced here: 352 us
  waiting for transfers between devices  183 us (52%)
  matrix products  96.2 us (27%)
  blocking collectives  35.9 us (10%)
  between operations  15.6 us (4%)
  other arithmetic  9.49 us (3%)
  starting transfers between devices  5.94 us (2%)
  local copies, waits for them, and re-layouts  5.78 us (2%)
    reduce_scatter x1, waiting for transfers between devices, on_device(): lax.psum_scatter(pieces.reshape(feats_owned * lax.axis_size('param'), exa...  140 us
    dot_general x8, matrix products, project_piece(): return jnp.dot(gradients, matrix, preferred_element_type=jnp.float32).T  79.4 us
    psum x1, waiting for transfers between devices, on_device(): fisher = lax.psum(partial_fisher, 'ex') / examples_total  42.4 us
    all_to_all x1, blocking collectives, on_device(): lax.all_to_all(conditioned, 'param', split_axis=1, concat_axis=0, tiled=T...  21.9 us
    all_to_all x1, blocking collectives, to_targets(): lax.all_to_all(partial_scores, 'param', split_axis=0, concat_axis=1, tile...  14 us
    dot_general x10, matrix products, newton_inverse(): jnp.einsum('bij,bjk->bik', damped, iterate, precision=lax.Precision.HIGHEST)  10.5 us
  transfers between devices with their start and end apart: 3, of which 3 were waited for; matrix products, arithmetic and copies ran while one was open for 0% of the time, Pallas kernels for 0%

commit v1 on v0

--- a/solution.py
+++ b/solution.py
@@ -75,7 +75,7 @@
     block_total = block_rows.shape[0] // BLOCK
     blocks = block_rows.reshape(block_total, BLOCK, exam_dev)
     partial_fisher = jnp.einsum("bie,bje->bij", blocks, blocks, preferred_element_type=jnp.float32)
-    fisher = lax.psum(partial_fisher, "ex") / examples_total
+    fisher = jnp.sum(lax.all_gather(partial_fisher, "ex"), axis=0) / examples_total
     inverse_bf = newton_inverse(fisher).astype(jnp.bfloat16)
     conditioned = jnp.einsum("bmj,bme->bje", inverse_bf, blocks, preferred_element_type=jnp.float32)
     conditioned = conditioned.astype(jnp.bfloat16).reshape(block_rows.shape[0], exam_dev)

time: 354 us -> 307 us (0.87)
  waiting for transfers between devices: 183 us -> 141 us
  matrix products: 96.2 us -> 87.2 us
  blocking collectives: 35.9 us -> 43.1 us
    psum x1 -> x0, waiting for transfers between devices: 42.4 us -> none  [on_device(): fisher = lax.psum(partial_fisher, 'ex') / examples_total]
    all_gather x0 -> x1, blocking collectives: none -> 10.3 us  [on_device(): lax.all_gather(partial_fisher, 'ex')]
    dot_general x10, matrix products: 10.5 us -> 2.08 us  [newton_inverse(): jnp.einsum('bij,bjk->bik', damped, iterate, precision=lax.Precision.HIGHEST)]
  transfers between devices with their start and end apart: 3 -> 2, of which waited for: 3 -> 2; matrix products, arithmetic and copies ran while one was open for 0% -> 0% of each run, Pallas kernels for 0% -> 0%
where the time goes in v1:
time: 307 us
  waiting for transfers between devices  141 us (46%)
  matrix products  87.2 us (28%)
  blocking collectives  43.1 us (14%)
  between operations  15.6 us (5%)
  other arithmetic  7.81 us (3%)
  starting transfers between devices  5.9 us (2%)
  local copies, waits for them, and re-layouts  5.78 us (2%)
    reduce_scatter x1, waiting for transfers between devices, on_device(): lax.psum_scatter(pieces.reshape(feats_owned * lax.axis_size('param'), exa...  140 us
    dot_general x8, matrix products, project_piece(): return jnp.dot(gradients, matrix, preferred_element_type=jnp.float32).T  79.4 us
    all_to_all x1, blocking collectives, on_device(): lax.all_to_all(conditioned, 'param', split_axis=1, concat_axis=0, tiled=T...  18.8 us
    all_to_all x1, blocking collectives, to_targets(): lax.all_to_all(partial_scores, 'param', split_axis=0, concat_axis=1, tile...  14 us
    all_gather x1, blocking collectives, on_device(): lax.all_gather(partial_fisher, 'ex')  10.3 us
  transfers between devices with their start and end apart: 2, of which 2 were waited for; matrix products, arithmetic and copies ran while one was open for 0% of the time, Pallas kernels for 0%

profile of v1, /device:TPU:1, one launch (start us, length us, event | category | flops | bytes accessed | tf_op | source)
XLA Modules:
  0.0 306.6 jit_solution(11893982916501771363)
XLA Ops:
  7.2 89.3 %while.12 = (s32[]{:T(128)}, f32[8,512,128]{2,1,0:T(8,128)}, s32[]{:T(128)}, s32[8]{0:T(128)S(1)}, s32[]{:T(128)}, /*index=5*/bf16[128,8192]{1,0:T(8,128)(2,1)}, s32[]{:T(128)}) while((s32[]{:T(128)}, f32[8,512,128]{2,1,0:T(8,128)}, s32[]{:T(128)}, s32[8]{0:T(128)S(1)}, s32[]{:T(128)}, /*index=5*/bf16[128,8192]{1,0:T(8,128)(2,1)}, ...), condition=%wide.region_1.2_spmd, body=%wide.region_0.1_spmd.sunk | while | flops 1128285184 | bytes 2430049 | solution.py:63
  7.2 0.6 dynamic_slice.9
  7.8 0.6 add_multiply_fusion.4
  8.4 9.9 %fusion.80 = f32[8,512,128]{2,1,0:T(8,128)} fusion(f32[8,512,128]{2,1,0:T(8,128)} %get-tuple-element.145, s32[]{:T(128)} %get-tuple-element.144, bf16[128,8192]{1,0:T(8,128)(2,1)} %get-tuple-element.156, s32[]{:T(128)} %get-tuple-element.155, s32[512]{0:T(512)S(1)} %add_multiply_fusion.4, s32[8192]{0:T(1024)S(1)} %add_multiply_fusion.5), kind=kOutput, calls=%fused_computation.11.clone.1 | convolution fusion | flops 1128267776 | bytes 2395136 | tf_op jit(solution)/shard_map/while/body/eval_jaxpr/dot_general | solution.py:60
  18.4 0.6 dynamic_slice.9
  18.9 0.6 add_multiply_fusion.4
  19.6 9.9 %fusion.80 = f32[8,512,128]{2,1,0:T(8,128)} fusion(f32[8,512,128]{2,1,0:T(8,128)} %get-tuple-element.145, s32[]{:T(128)} %get-tuple-element.144, bf16[128,8192]{1,0:T(8,128)(2,1)} %get-tuple-element.156, s32[]{:T(128)} %get-tuple-element.155, s32[512]{0:T(512)S(1)} %add_multiply_fusion.4, s32[8192]{0:T(1024)S(1)} %add_multiply_fusion.5), kind=kOutput, calls=%fused_computation.11.clone.1 | convolution fusion | flops 1128267776 | bytes 2395136 | tf_op jit(solution)/shard_map/while/body/eval_jaxpr/dot_general | solution.py:60
  29.5 0.6 dynamic_slice.9
  30.1 0.6 add_multiply_fusion.4
  30.7 9.9 %fusion.80 = f32[8,512,128]{2,1,0:T(8,128)} fusion(f32[8,512,128]{2,1,0:T(8,128)} %get-tuple-element.145, s32[]{:T(128)} %get-tuple-element.144, bf16[128,8192]{1,0:T(8,128)(2,1)} %get-tuple-element.156, s32[]{:T(128)} %get-tuple-element.155, s32[512]{0:T(512)S(1)} %add_multiply_fusion.4, s32[8192]{0:T(1024)S(1)} %add_multiply_fusion.5), kind=kOutput, calls=%fused_computation.11.clone.1 | convolution fusion | flops 1128267776 | bytes 2395136 | tf_op jit(solution)/shard_map/while/body/eval_jaxpr/dot_general | solution.py:60
  40.7 0.6 dynamic_slice.9
  41.2 0.6 add_multiply_fusion.4
  41.9 9.9 %fusion.80 = f32[8,512,128]{2,1,0:T(8,128)} fusion(f32[8,512,128]{2,1,0:T(8,128)} %get-tuple-element.145, s32[]{:T(128)} %get-tuple-element.144, bf16[128,8192]{1,0:T(8,128)(2,1)} %get-tuple-element.156, s32[]{:T(128)} %get-tuple-element.155, s32[512]{0:T(512)S(1)} %add_multiply_fusion.4, s32[8192]{0:T(1024)S(1)} %add_multiply_fusion.5), kind=kOutput, calls=%fused_computation.11.clone.1 | convolution fusion | flops 1128267776 | bytes 2395136 | tf_op jit(solution)/shard_map/while/body/eval_jaxpr/dot_general | solution.py:60
  51.8 0.6 dynamic_slice.9
  52.4 0.6 add_multiply_fusion.4
  53.0 9.9 %fusion.80 = f32[8,512,128]{2,1,0:T(8,128)} fusion(f32[8,512,128]{2,1,0:T(8,128)} %get-tuple-element.145, s32[]{:T(128)} %get-tuple-element.144, bf16[128,8192]{1,0:T(8,128)(2,1)} %get-tuple-element.156, s32[]{:T(128)} %get-tuple-element.155, s32[512]{0:T(512)S(1)} %add_multiply_fusion.4, s32[8192]{0:T(1024)S(1)} %add_multiply_fusion.5), kind=kOutput, calls=%fused_computation.11.clone.1 | convolution fusion | flops 1128267776 | bytes 2395136 | tf_op jit(solution)/shard_map/while/body/eval_jaxpr/dot_general | solution.py:60
  63.0 0.6 dynamic_slice.9
  63.6 0.6 add_multiply_fusion.4
  64.2 9.9 %fusion.80 = f32[8,512,128]{2,1,0:T(8,128)} fusion(f32[8,512,128]{2,1,0:T(8,128)} %get-tuple-element.145, s32[]{:T(128)} %get-tuple-element.144, bf16[128,8192]{1,0:T(8,128)(2,1)} %get-tuple-element.156, s32[]{:T(128)} %get-tuple-element.155, s32[512]{0:T(512)S(1)} %add_multiply_fusion.4, s32[8192]{0:T(1024)S(1)} %add_multiply_fusion.5), kind=kOutput, calls=%fused_computation.11.clone.1 | convolution fusion | flops 1128267776 | bytes 2395136 | tf_op jit(solution)/shard_map/while/body/eval_jaxpr/dot_general | solution.py:60
  74.2 0.6 dynamic_slice.9
  74.7 0.6 add_multiply_fusion.4
  75.4 9.9 %fusion.80 = f32[8,512,128]{2,1,0:T(8,128)} fusion(f32[8,512,128]{2,1,0:T(8,128)} %get-tuple-element.145, s32[]{:T(128)} %get-tuple-element.144, bf16[128,8192]{1,0:T(8,128)(2,1)} %get-tuple-element.156, s32[]{:T(128)} %get-tuple-element.155, s32[512]{0:T(512)S(1)} %add_multiply_fusion.4, s32[8192]{0:T(1024)S(1)} %add_multiply_fusion.5), kind=kOutput, calls=%fused_computation.11.clone.1 | convolution fusion | flops 1128267776 | bytes 2395136 | tf_op jit(solution)/shard_map/while/body/eval_jaxpr/dot_general | solution.py:60
  85.3 0.6 dynamic_slice.9
  85.9 0.6 add_multiply_fusion.4
  86.5 9.9 %fusion.80 = f32[8,512,128]{2,1,0:T(8,128)} fusion(f32[8,512,128]{2,1,0:T(8,128)} %get-tuple-element.145, s32[]{:T(128)} %get-tuple-element.144, bf16[128,8192]{1,0:T(8,128)(2,1)} %get-tuple-element.156, s32[]{:T(128)} %get-tuple-element.155, s32[512]{0:T(512)S(1)} %add_multiply_fusion.4, s32[8192]{0:T(1024)S(1)} %add_multiply_fusion.5), kind=kOutput, calls=%fused_computation.11.clone.1 | convolution fusion | flops 1128267776 | bytes 2395136 | tf_op jit(solution)/shard_map/while/body/eval_jaxpr/dot_general | solution.py:60
  96.5 0.0 reduce-scatter.2.cloned.1.call-update
  96.5 140.3 %reduce-scatter.2.cloned.1.call-done = f32[64,128]{1,0:T(8,128)} async-done(((f32[4096,128]{1,0:T(8,128)}), f32[64,128]{1,0:T(8,128)}) %reduce-scatter.2.cloned.1.call-update) | async-done | bytes 32784 | tf_op jit(solution)/shard_map/reduce_scatter | solution.py:64
  236.7 0.8 convert_element_type.49
  237.5 5.9 %collective-permute-start = (bf16[64,128]{1,0:T(8,128)(2,1)S(1)}, bf16[64,128]{1,0:T(8,128)(2,1)S(1)}, u32[]{:S(2)}, u32[]{:S(2)}) collective-permute-start(bf16[64,128]{1,0:T(8,128)(2,1)S(1)} %convert_element_type.49), channel_id=1, source_target_pairs={{0,4},{4,0},{8,12},{12,8},{16,20},{20,16},{24,28},{28,24},{32,36},... | collective-permute-start | bytes 49160 | tf_op jit(solution)/shard_map/ppermute | solution.py:14
  243.4 0.8 collective-permute-done
  244.2 0.8 broadcast_select_fusion.1
  245.0 0.1 fusion.30
  245.1 10.3 %all-gather = f32[512,128]{1,0:T(8,128)S(1)} all-gather(f32[128,128]{1,0:T(8,128)S(1)} %fusion.30), channel_id=2, replica_groups=mesh['param'=64,'ex'=4] {'ex'}, dimensions={0}, use_global_device_ids=true | all-gather | bytes 327680 | tf_op jit(solution)/shard_map/all_gather | solution.py:78
  255.5 0.6 select_reduce_fusion.1
  256.8 0.6 select_reduce_fusion
  258.1 0.2 convolution_subtract_fusion.9
  258.3 0.2 fusion.22
  258.5 0.2 convolution_subtract_fusion.8
  258.7 0.2 fusion.35
  258.9 0.2 convolution_subtract_fusion.7
  259.2 0.2 fusion.36
  259.4 0.2 convolution_subtract_fusion.6
  259.6 0.2 fusion.37
  259.8 0.2 convolution_subtract_fusion.5
  260.0 0.2 fusion.38
  260.2 0.2 convolution_subtract_fusion.4
  260.4 0.2 fusion.39
  260.6 0.2 convolution_subtract_fusion.3
  260.9 0.2 fusion.40
  261.1 0.2 convolution_subtract_fusion.2
  261.3 0.2 fusion.41
  261.5 0.2 convolution_subtract_fusion.1
  261.7 0.2 fusion.42
  261.9 0.2 convolution_subtract_fusion
  262.1 0.2 convolution_convert_fusion
  262.3 0.2 fusion.29
  262.6 0.1 copy.9
  262.7 18.8 %all_to_all.38 = bf16[64,64,2]{0,2,1:T(2,128)(2,1)S(1)} all-to-all(bf16[64,64,2]{0,2,1:T(2,128)(2,1)S(1)} %bitcast.60), channel_id=1, replica_groups=mesh['param'=64,'ex'=4] {'param'}, dimensions={1} | all-to-all | bytes 32768 | tf_op jit(solution)/shard_map/all_to_all | solution.py:83
  281.5 0.1 all_to_all.31
  281.6 3.4 %convolution_bitcast_fusion = f32[512,2]{0,1:T(2,128)S(1)} fusion(bf16[4096,2]{0,1:T(2,128)(2,1)S(1)} %all_to_all.31, bf16[512,4096]{1,0:T(8,128)(2,1)} %param.7), kind=kOutput, calls=%fused_computation.32 | convolution fusion | flops 8388608 | bytes 4214784 | tf_op jit(solution)/shard_map/dot_general | solution.py:84
  284.9 0.1 all_to_all.32
  285.0 0.1 copy.11
  285.1 14.0 %all_to_all.39 = f32[64,8,2]{1,2,0:T(2,128)S(1)} all-to-all(f32[64,8,2]{1,2,0:T(2,128)S(1)} %copy.11), channel_id=1, replica_groups=mesh['param'=64,'ex'=4] {'param'}, dimensions={0} | all-to-all | bytes 8192 | tf_op jit(solution)/shard_map/all_to_all | solution.py:44
  299.1 0.7 copy.12
  (14 shorter events, 0.1 us)
Async XLA Ops:
  6.5 230.2 %reduce-scatter.2.cloned.1.call-start = ((), (), s32[]{:S(2)}) async-start(), calls=%async_computation.3 | async-start | bytes 2129920 | tf_op jit(solution)/shard_map/reduce_scatter | solution.py:64
  237.5 6.7 %collective-permute-start = (bf16[64,128]{1,0:T(8,128)(2,1)S(1)}, bf16[64,128]{1,0:T(8,128)(2,1)S(1)}, u32[]{:S(2)}, u32[]{:S(2)}) collective-permute-start(bf16[64,128]{1,0:T(8,128)(2,1)S(1)} %convert_element_type.49), channel_id=1, source_target_pairs={{0,4},{4,0},{8,12},{12,8},{16,20},{20,16},{24,28},{28,24},{32,36},... | collective-permute-start | bytes 49160 | tf_op jit(solution)/shard_map/ppermute | solution.py:14
Sparse Core Ops, SparseCore 0:
  96.6 140.0 reduce-scatter.1
